TPU v7x, 32 devices: a whole 2x2x4 slice. The times are simulated.
32 devices in a mesh: region: 8 (over y, x, core), brick: 4 (over z).
Axes of the slice: x: 2, y: 2, z: 4, core: 2. Of those that a mesh axis runs over, the one named last changes fastest.
Arguments:
- velocity: float32 [3, 128, 64, 256], P(None, 'region', 'brick'), may hold values from -6 to 6
- viscosity: float32 [128, 64, 256], P('region', 'brick'), may hold values from 0.05 to 0.5
- marker_pos: float32 [3, 131072], P(None, ('region', 'brick')), as said below
- marker_force: float32 [3, 131072], P(None, ('region', 'brick')), may hold values from -240 to 240
- slot_lists: int32 [32, 8192], P(('region', 'brick')), may hold values from 0 to 16384, as said below
Outputs:
- predicted: float32 [3, 128, 64, 256], P(None, 'region', 'brick')
Inputs may be any that keep to these rules, and one draw needn't show every extreme that they name: `slot_lists`: each row lists, in increasing order, the indices within its region group's 16384 markers of the markers whose second coordinate lies in that brick's rows, then is padded with 16384; every marker of the group stands in exactly one row, and in every region group one row is full. `marker_pos`: the first coordinate of a marker lies 2 or more cells inside its region group's slab, the third 2 or more cells from the grid's ends, and the second within the rows of the brick whose slot row lists it.
All inputs are finite; a program needn't handle non-finite values.
Results may differ from a plain program's by a relative error of at most 0.00088.
Values sent between devices are 32-bit elements; how exact they have to be, the bound alone decides.
No kernel may reach another device: no remote copies, remote signals or barrier semaphores. Data moves between devices by JAX's collectives and lax.ppermute only.
A program may use at most 192 MiB of HBM per device.

v0:
```python
import jax
import jax.numpy as jnp
from jax import lax
from jax.sharding import PartitionSpec as P


def from_behind(x, axis, by):
    peers = lax.axis_size(axis)
    pairs = [(i, i + by) for i in range(peers) if 0 <= i + by < peers]
    return lax.ppermute(x, axis, pairs)


def extended_2(block, sides, width):
    for axis, dim in sides:
        count = lax.axis_size(axis)
        forward = [(i, i + 1) for i in range(count - 1)]
        backward = [(target, source) for source, target in forward]
        low = lax.ppermute(
            lax.slice_in_dim(block, block.shape[dim] - width, None, axis=dim), axis, forward
        )
        high = lax.ppermute(lax.slice_in_dim(block, 0, width, axis=dim), axis, backward)
        block = jnp.concatenate([low, block, high], axis=dim)
    return block


def kernel_weight(dist):
    return jnp.where(jnp.abs(dist) < 2.0, 0.25 * (1.0 + jnp.cos(0.5 * jnp.pi * dist)), 0.0)


def spread_rows(pos, force, row_low, rows, col_low, cols, depth):
    count = pos.shape[1]
    block = 1024
    x_centre = (col_low + jnp.arange(cols, dtype=jnp.int32)).astype(jnp.float32) + 0.5
    y_centre = (row_low + jnp.arange(rows, dtype=jnp.int32)).astype(jnp.float32) + 0.5
    z_centre = jnp.arange(depth, dtype=jnp.int32).astype(jnp.float32) + 0.5

    def one_block(turn, total):
        start = turn * block
        pos_part = lax.dynamic_slice_in_dim(pos, start, block, 1)
        force_part = lax.dynamic_slice_in_dim(force, start, block, 1)
        weight_x = kernel_weight(x_centre[:, None] - pos_part[0][None, :])
        weight_y = kernel_weight(y_centre[:, None] - pos_part[1][None, :])
        weight_z = kernel_weight(z_centre[None, :] - pos_part[2][:, None])
        factor = (
            force_part[:, None, None, :] * weight_x[None, :, None, :] * weight_y[None, None, :, :]
        )
        factor = factor.reshape(3 * cols * rows, block).astype(jnp.bfloat16)
        return total + jnp.dot(
            factor, weight_z.astype(jnp.bfloat16), preferred_element_type=jnp.float32
        )

    empty = jnp.zeros((3 * cols * rows, depth), jnp.float32)
    total = lax.fori_loop(0, count // block, one_block, empty)
    return total.reshape(3, cols, rows, depth)


def side(array, axis, offset):
    parts = [slice(1, -1), slice(1, -1), slice(1, -1)]
    size = array.shape[array.ndim - 3 + axis]
    parts[axis] = slice(1 + offset, size - 1 + offset)
    if array.ndim == 4:
        return array[:, parts[0], parts[1], parts[2]]
    return array[parts[0], parts[1], parts[2]]


def advance(padded, force_field):
    vel = padded[:3]
    visc = padded[3]
    speed = side(vel, 0, 0)
    visc_mid = side(visc, 0, 0)
    diffusion = jnp.zeros_like(speed)
    advection = jnp.zeros_like(speed)
    for axis in range(3):
        upper = side(vel, axis, 1)
        lower = side(vel, axis, -1)
        visc_up = side(visc, axis, 1)
        visc_dn = side(visc, axis, -1)
        diffusion = (
            diffusion
            + 0.5 * (visc_mid + visc_up) * (upper - speed)
            - 0.5 * (visc_mid + visc_dn) * (speed - lower)
        )
        advection = advection + speed[axis][None] * (upper - lower) * 0.5
    return speed + 0.1 * (diffusion - advection + force_field)


def body(velocity, viscosity, marker_pos, marker_force, slot_lists):
    cols, own_rows, depth = viscosity.shape
    region = lax.axis_index("region")
    brick = lax.axis_index("brick")
    own_slots = slot_lists[0]
    row_low = brick * own_rows - 2
    rows = own_rows + 4
    blank = jnp.zeros((3, own_slots.shape[0]), jnp.float32)
    start = jnp.int32(0)
    pos_piece = lax.all_gather(marker_pos, "brick", axis=1, tiled=True)
    force_piece = lax.all_gather(marker_force, "brick", axis=1, tiled=True)
    length = pos_piece.shape[1]
    inside = ((own_slots >= start) & (own_slots < start + length))[None, :]
    local = jnp.clip(own_slots, 0, length - 1)
    pos = jnp.where(inside, jnp.take(pos_piece, local, axis=1), blank)
    force = jnp.where(inside, jnp.take(force_piece, local, axis=1), blank)
    field = spread_rows(pos, force, row_low, rows, region * cols, cols, depth)
    upper_rim = field[:, :, own_rows + 2 :, :]
    lower_rim = field[:, :, :2, :]
    from_below = from_behind(upper_rim, "brick", 1)
    from_above = from_behind(lower_rim, "brick", -1)
    centre = field[:, :, 2 : own_rows + 2, :]
    centre = centre.at[:, :, :2, :].add(from_below)
    force_field = centre.at[:, :, own_rows - 2 :, :].add(from_above)
    stacked = jnp.concatenate([velocity, viscosity[None]], axis=0)
    extended = extended_2(stacked, (("region", 1), ("brick", 2)), 1)
    padded = jnp.pad(extended, ((0, 0), (0, 0), (0, 0), (1, 1)))
    return advance(padded, force_field)


def solution(mesh):
    placed = (
        P(None, "region", "brick", None),
        P("region", "brick", None),
        P(None, ("region", "brick")),
        P(None, ("region", "brick")),
        P(("region", "brick"), None),
    )
    return jax.shard_map(
        body,
        mesh=mesh,
        in_specs=placed,
        out_specs=P(None, "region", "brick", None),
        check_vma=False,
    )
```

profile of v0, /device:TPU:19, one launch (start us, length us, event | category | flops | bytes accessed | tf_op | source)
XLA Modules:
  0.0 469.4 jit_solution(8026704652510305181)
XLA Ops:
  0.0 0.8 broadcast_clamp_fusion
  0.8 0.9 and_reduce_fusion
  1.7 1.5 copy.10
  3.2 137.8 %all_gather.6 = f32[3,16384]{0,1:T(8,128)} all-gather(f32[3,4096]{0,1:T(8,128)S(1)} %copy.10), channel_id=1, replica_groups=mesh['region'=8,'brick'=4] {'brick'}, dimensions={1}, use_global_device_ids=true | all-gather | bytes 245760 | tf_op jit(solution)/shard_map/all_gather | solution.py:97
  141.0 0.6 copy.11
  141.7 138.8 %all_gather.7 = f32[3,16384]{0,1:T(8,128)} all-gather(f32[3,4096]{0,1:T(8,128)S(1)} %copy.11), channel_id=1, replica_groups=mesh['region'=8,'brick'=4] {'brick'}, dimensions={1}, use_global_device_ids=true | all-gather | bytes 245760 | tf_op jit(solution)/shard_map/all_gather | solution.py:96
  280.4 31.2 %gather_fusion = f32[8192,3]{1,0:T(8,128)} fusion(f32[3,16384]{0,1:T(8,128)} %all_gather.6, s32[8192]{0:T(1024)S(1)} %fusion.44), kind=kCustom, calls=%fused_computation.clone | custom fusion | bytes 229376 | tf_op jit(solution)/shard_map/jit(_take)/gather | solution.py:102
  311.7 31.3 %gather_fusion.1 = f32[8192,3]{1,0:T(8,128)} fusion(f32[3,16384]{0,1:T(8,128)} %all_gather.7, s32[8192]{0:T(1024)S(1)} %fusion.44), kind=kCustom, calls=%fused_computation.1.clone | custom fusion | bytes 229376 | tf_op jit(solution)/shard_map/jit(_take)/gather | solution.py:101
  342.9 8.0 %bitcast_select_fusion = (f32[3,8192]{0,1:T(8,128)}, f32[3,8192]{0,1:T(8,128)}) fusion(f32[8192,3]{1,0:T(8,128)} %gather_fusion.1, pred[8192]{0:T(1024)(128)(4,1)S(1)} %compare_and_fusion, pred[8192]{0:T(1024)(128)(4,1)S(1)} %and_reduce_fusion, f32[8192,3]{1,0:T(8,128)} %gather_fusion), kind=kLoop, calls=%fused_computation.47 | loop fusion | flops 98304 | bytes 409600 | tf_op jit(solution)/shard_map/jit(_where)/select_n | solution.py:101
  350.9 2.8 copy.12
  353.8 2.9 copy.13
  356.6 79.9 %while.16 = (s32[]{:T(128)}, f32[960,256]{1,0:T(8,128)S(1)}, f32[3,8192]{1,0:T(4,128)S(1)}, f32[3,8192]{1,0:T(4,128)S(1)}, s32[]{:T(128)}, /*index=5*/s32[]{:T(1...) while((s32[]{:T(128)}, f32[960,256]{1,0:T(8,128)S(1)}, ...), condition=%wide.region_1.3_spmd.clone, body=%wide.region_0.2_spmd.clone.sunk | while | flops 508179072 | bytes 11381301 | solution.py:53
  357.3 0.4 fusion.56
  357.7 0.6 multiply_convert_fusion.2
  358.3 2.0 convert_element_type.63
  360.3 6.2 %convolution_add_fusion.2 = f32[960,256]{1,0:T(8,128)S(1)} fusion(bf16[960,1024]{1,0:T(8,128)(2,1)} %convert_element_type.63, f32[960,256]{1,0:T(8,128)S(1)} %get-tuple-element.284, f32[1024]{0:T(1024)S(1)} %bitcast.34, f32[256]{0:T(256)S(1)} %convert_add_fusion.8, pred[]{:T(512)S(6)} %compare.35), kind=kOutput, calls=%fused_computation.8.clone.1 | convolution fusion | flops 505905152 | bytes 3937281 | tf_op jit(solution)/shard_map/while/body/eval_jaxpr/dot_general | solution.py:48
  367.7 0.6 multiply_convert_fusion.2
  368.3 2.0 convert_element_type.63
  370.3 6.2 %convolution_add_fusion.2 = f32[960,256]{1,0:T(8,128)S(1)} fusion(bf16[960,1024]{1,0:T(8,128)(2,1)} %convert_element_type.63, f32[960,256]{1,0:T(8,128)S(1)} %get-tuple-element.284, f32[1024]{0:T(1024)S(1)} %bitcast.34, f32[256]{0:T(256)S(1)} %convert_add_fusion.8, pred[]{:T(512)S(6)} %compare.35), kind=kOutput, calls=%fused_computation.8.clone.1 | convolution fusion | flops 505905152 | bytes 3937281 | tf_op jit(solution)/shard_map/while/body/eval_jaxpr/dot_general | solution.py:48
  377.7 0.6 multiply_convert_fusion.2
  378.3 2.0 convert_element_type.63
  380.3 6.3 %convolution_add_fusion.2 = f32[960,256]{1,0:T(8,128)S(1)} fusion(bf16[960,1024]{1,0:T(8,128)(2,1)} %convert_element_type.63, f32[960,256]{1,0:T(8,128)S(1)} %get-tuple-element.284, f32[1024]{0:T(1024)S(1)} %bitcast.34, f32[256]{0:T(256)S(1)} %convert_add_fusion.8, pred[]{:T(512)S(6)} %compare.35), kind=kOutput, calls=%fused_computation.8.clone.1 | convolution fusion | flops 505905152 | bytes 3937281 | tf_op jit(solution)/shard_map/while/body/eval_jaxpr/dot_general | solution.py:48
  387.7 0.6 multiply_convert_fusion.2
  388.3 2.0 convert_element_type.63
  390.3 6.2 %convolution_add_fusion.2 = f32[960,256]{1,0:T(8,128)S(1)} fusion(bf16[960,1024]{1,0:T(8,128)(2,1)} %convert_element_type.63, f32[960,256]{1,0:T(8,128)S(1)} %get-tuple-element.284, f32[1024]{0:T(1024)S(1)} %bitcast.34, f32[256]{0:T(256)S(1)} %convert_add_fusion.8, pred[]{:T(512)S(6)} %compare.35), kind=kOutput, calls=%fused_computation.8.clone.1 | convolution fusion | flops 505905152 | bytes 3937281 | tf_op jit(solution)/shard_map/while/body/eval_jaxpr/dot_general | solution.py:48
  397.7 0.6 multiply_convert_fusion.2
  398.3 2.0 convert_element_type.63
  400.3 6.3 %convolution_add_fusion.2 = f32[960,256]{1,0:T(8,128)S(1)} fusion(bf16[960,1024]{1,0:T(8,128)(2,1)} %convert_element_type.63, f32[960,256]{1,0:T(8,128)S(1)} %get-tuple-element.284, f32[1024]{0:T(1024)S(1)} %bitcast.34, f32[256]{0:T(256)S(1)} %convert_add_fusion.8, pred[]{:T(512)S(6)} %compare.35), kind=kOutput, calls=%fused_computation.8.clone.1 | convolution fusion | flops 505905152 | bytes 3937281 | tf_op jit(solution)/shard_map/while/body/eval_jaxpr/dot_general | solution.py:48
  407.7 0.6 multiply_convert_fusion.2
  408.3 2.0 convert_element_type.63
  410.3 6.3 %convolution_add_fusion.2 = f32[960,256]{1,0:T(8,128)S(1)} fusion(bf16[960,1024]{1,0:T(8,128)(2,1)} %convert_element_type.63, f32[960,256]{1,0:T(8,128)S(1)} %get-tuple-element.284, f32[1024]{0:T(1024)S(1)} %bitcast.34, f32[256]{0:T(256)S(1)} %convert_add_fusion.8, pred[]{:T(512)S(6)} %compare.35), kind=kOutput, calls=%fused_computation.8.clone.1 | convolution fusion | flops 505905152 | bytes 3937281 | tf_op jit(solution)/shard_map/while/body/eval_jaxpr/dot_general | solution.py:48
  417.7 0.6 multiply_convert_fusion.2
  418.3 2.0 convert_element_type.63
  420.3 6.2 %convolution_add_fusion.2 = f32[960,256]{1,0:T(8,128)S(1)} fusion(bf16[960,1024]{1,0:T(8,128)(2,1)} %convert_element_type.63, f32[960,256]{1,0:T(8,128)S(1)} %get-tuple-element.284, f32[1024]{0:T(1024)S(1)} %bitcast.34, f32[256]{0:T(256)S(1)} %convert_add_fusion.8, pred[]{:T(512)S(6)} %compare.35), kind=kOutput, calls=%fused_computation.8.clone.1 | convolution fusion | flops 505905152 | bytes 3937281 | tf_op jit(solution)/shard_map/while/body/eval_jaxpr/dot_general | solution.py:48
  427.7 0.6 multiply_convert_fusion.2
  428.3 2.0 convert_element_type.63
  430.3 6.3 %convolution_add_fusion.2 = f32[960,256]{1,0:T(8,128)S(1)} fusion(bf16[960,1024]{1,0:T(8,128)(2,1)} %convert_element_type.63, f32[960,256]{1,0:T(8,128)S(1)} %get-tuple-element.284, f32[1024]{0:T(1024)S(1)} %bitcast.34, f32[256]{0:T(256)S(1)} %convert_add_fusion.8, pred[]{:T(512)S(6)} %compare.35), kind=kOutput, calls=%fused_computation.8.clone.1 | convolution fusion | flops 505905152 | bytes 3937281 | tf_op jit(solution)/shard_map/while/body/eval_jaxpr/dot_general | solution.py:48
  436.8 4.9 %collective-permute-start.4 = (f32[3,16,2,256]{3,2,1,0:T(2,128)S(1)}, f32[3,16,2,256]{3,2,1,0:T(2,128)S(1)}, u32[]{:S(2)}, u32[]{:S(2)}) collective-permute-start(f32[3,16,2,256]{3,2,1,0:T(2,128)S(1)} %get-tuple-element.214), channel_id=1, source_target_pairs={{0,1},{1,2},{2,3},{4,5},{5,6},{6,7},{8,9},{9,10},{10,11},{12,13},{... | collective-permute-start | bytes 294920 | tf_op jit(solution)/shard_map/ppermute | solution.py:10
  441.7 1.9 collective-permute-start.5
  443.7 5.7 %collective-permute-start = (f32[4,1,16,256]{3,2,1,0:T(8,128)S(1)}, f32[4,1,16,256]{3,2,1,0:T(8,128)S(1)}, u32[]{:S(2)}, u32[]{:S(2)}) collective-permute-start(f32[4,1,16,256]{3,2,1,0:T(8,128)S(1)} %get-tuple-element.215), channel_id=1, source_target_pairs={{0,4},{4,8},{8,12},{12,16},{16,20},{20,24},{24,28},{1,5},{5,9},{9,... | collective-permute-start | bytes 196616 | tf_op jit(solution)/shard_map/ppermute | solution.py:18
  449.3 1.9 collective-permute-start.1
  451.4 4.4 collective-permute-done.1
  455.9 3.6 collective-permute-start.2
  459.6 2.1 collective-permute-start.3
  461.9 2.7 collective-permute-done.3
  464.7 1.3 select_maximum_fusion
  466.1 0.5 fusion.41
  466.6 2.8 multiply_add_fusion
  (117 shorter events, 8.6 us)
Async XLA Ops:
  3.2 137.8 %copy-start.4 = (f32[3,4096]{1,0:T(4,128)S(1)}, f32[3,4096]{1,0:T(4,128)}, u32[]{:S(2)}) copy-start(f32[3,4096]{1,0:T(4,128)} %param.15) | copy-start | bytes 147460
  356.6 0.7 copy-start.2
  360.3 6.3 %copy-start.3 = (f32[3,8192]{1,0:T(4,128)S(1)}, f32[3,8192]{1,0:T(4,128)}, u32[]{:S(2)}) copy-start(f32[3,8192]{1,0:T(4,128)} %copy-done.2) | copy-start | bytes 294916 | tf_op jit(solution)/shard_map/while
  366.6 0.7 copy-start.2
  370.3 6.3 %copy-start.3 = (f32[3,8192]{1,0:T(4,128)S(1)}, f32[3,8192]{1,0:T(4,128)}, u32[]{:S(2)}) copy-start(f32[3,8192]{1,0:T(4,128)} %copy-done.2) | copy-start | bytes 294916 | tf_op jit(solution)/shard_map/while
  376.6 0.7 copy-start.2
  380.3 6.3 %copy-start.3 = (f32[3,8192]{1,0:T(4,128)S(1)}, f32[3,8192]{1,0:T(4,128)}, u32[]{:S(2)}) copy-start(f32[3,8192]{1,0:T(4,128)} %copy-done.2) | copy-start | bytes 294916 | tf_op jit(solution)/shard_map/while
  386.6 0.7 copy-start.2
  390.3 6.3 %copy-start.3 = (f32[3,8192]{1,0:T(4,128)S(1)}, f32[3,8192]{1,0:T(4,128)}, u32[]{:S(2)}) copy-start(f32[3,8192]{1,0:T(4,128)} %copy-done.2) | copy-start | bytes 294916 | tf_op jit(solution)/shard_map/while
  396.6 0.7 copy-start.2
  400.3 6.3 %copy-start.3 = (f32[3,8192]{1,0:T(4,128)S(1)}, f32[3,8192]{1,0:T(4,128)}, u32[]{:S(2)}) copy-start(f32[3,8192]{1,0:T(4,128)} %copy-done.2) | copy-start | bytes 294916 | tf_op jit(solution)/shard_map/while
  406.6 0.7 copy-start.2
  410.3 6.3 %copy-start.3 = (f32[3,8192]{1,0:T(4,128)S(1)}, f32[3,8192]{1,0:T(4,128)}, u32[]{:S(2)}) copy-start(f32[3,8192]{1,0:T(4,128)} %copy-done.2) | copy-start | bytes 294916 | tf_op jit(solution)/shard_map/while
  416.6 0.7 copy-start.2
  420.3 6.3 %copy-start.3 = (f32[3,8192]{1,0:T(4,128)S(1)}, f32[3,8192]{1,0:T(4,128)}, u32[]{:S(2)}) copy-start(f32[3,8192]{1,0:T(4,128)} %copy-done.2) | copy-start | bytes 294916 | tf_op jit(solution)/shard_map/while
  426.6 0.7 copy-start.2
  430.3 6.3 %copy-start.3 = (f32[3,8192]{1,0:T(4,128)S(1)}, f32[3,8192]{1,0:T(4,128)}, u32[]{:S(2)}) copy-start(f32[3,8192]{1,0:T(4,128)} %copy-done.2) | copy-start | bytes 294916 | tf_op jit(solution)/shard_map/while
  436.6 7.1 %copy-start = (f32[3,16,16,256]{3,2,1,0:T(8,128)S(1)}, f32[3,16,16,256]{3,2,1,0:T(8,128)}, u32[]{:S(2)}) copy-start(f32[3,16,16,256]{3,2,1,0:T(8,128)} %param.13) | copy-start | bytes 2359300
  436.6 7.1 %copy-start.1 = (f32[16,16,256]{2,1,0:T(8,128)S(1)}, f32[16,16,256]{2,1,0:T(8,128)}, u32[]{:S(2)}) copy-start(f32[16,16,256]{2,1,0:T(8,128)} %param.14) | copy-start | bytes 786436
  436.8 24.9 %collective-permute-start.4 = (f32[3,16,2,256]{3,2,1,0:T(2,128)S(1)}, f32[3,16,2,256]{3,2,1,0:T(2,128)S(1)}, u32[]{:S(2)}, u32[]{:S(2)}) collective-permute-start(f32[3,16,2,256]{3,2,1,0:T(2,128)S(1)} %get-tuple-element.214), channel_id=1, source_target_pairs={{0,1},{1,2},{2,3},{4,5},{5,6},{6,7},{8,9},{9,10},{10,11},{12,13},{... | collective-permute-start | bytes 294920 | tf_op jit(solution)/shard_map/ppermute | solution.py:10
  441.7 20.1 %collective-permute-start.5 = (f32[3,16,2,256]{3,2,1,0:T(2,128)S(1)}, f32[3,16,2,256]{3,2,1,0:T(2,128)S(1)}, u32[]{:S(2)}, u32[]{:S(2)}) collective-permute-start(f32[3,16,2,256]{3,2,1,0:T(2,128)S(1)} %get-tuple-element.213), channel_id=1, source_target_pairs={{1,0},{2,1},{3,2},{5,4},{6,5},{7,6},{9,8},{10,9},{11,10},{13,12},{... | collective-permute-start | bytes 294920 | tf_op jit(solution)/shard_map/ppermute | solution.py:10
  443.7 7.8 %collective-permute-start = (f32[4,1,16,256]{3,2,1,0:T(8,128)S(1)}, f32[4,1,16,256]{3,2,1,0:T(8,128)S(1)}, u32[]{:S(2)}, u32[]{:S(2)}) collective-permute-start(f32[4,1,16,256]{3,2,1,0:T(8,128)S(1)} %get-tuple-element.215), channel_id=1, source_target_pairs={{0,4},{4,8},{8,12},{12,16},{16,20},{20,24},{24,28},{1,5},{5,9},{9,... | collective-permute-start | bytes 196616 | tf_op jit(solution)/shard_map/ppermute | solution.py:18
  449.3 6.5 %collective-permute-start.1 = (f32[4,1,16,256]{3,2,1,0:T(8,128)S(1)}, f32[4,1,16,256]{3,2,1,0:T(8,128)S(1)}, u32[]{:S(2)}, u32[]{:S(2)}) collective-permute-start(f32[4,1,16,256]{3,2,1,0:T(8,128)S(1)} %get-tuple-element.216), channel_id=1, source_target_pairs={{4,0},{8,4},{12,8},{16,12},{20,16},{24,20},{28,24},{5,1},{9,5},{13... | collective-permute-start | bytes 196616 | tf_op jit(solution)/shard_map/ppermute | solution.py:21
  455.9 6.0 %collective-permute-start.2 = (f32[4,18,1,256]{3,2,1,0:T(1,128)S(1)}, f32[4,18,1,256]{3,2,1,0:T(1,128)S(1)}, u32[]{:S(2)}, u32[]{:S(2)}) collective-permute-start(f32[4,18,1,256]{3,2,1,0:T(1,128)S(1)} %get-tuple-element.211), channel_id=1, source_target_pairs={{0,1},{1,2},{2,3},{4,5},{5,6},{6,7},{8,9},{9,10},{10,11},{12,13},{... | collective-permute-start | bytes 221192 | tf_op jit(solution)/shard_map/ppermute | solution.py:18
  459.6 5.1 %collective-permute-start.3 = (f32[4,18,1,256]{3,2,1,0:T(1,128)S(1)}, f32[4,18,1,256]{3,2,1,0:T(1,128)S(1)}, u32[]{:S(2)}, u32[]{:S(2)}) collective-permute-start(f32[4,18,1,256]{3,2,1,0:T(1,128)S(1)} %get-tuple-element.212), channel_id=1, source_target_pairs={{1,0},{2,1},{3,2},{5,4},{6,5},{7,6},{9,8},{10,9},{11,10},{13,12},{... | collective-permute-start | bytes 221192 | tf_op jit(solution)/shard_map/ppermute | solution.py:21
where the time goes:
time: 470 us; the launch traced here: 469 us
  blocking collectives  277 us (59%)
  local copies, waits for them, and re-layouts  88.8 us (19%)
  matrix products  50 us (11%)
  other arithmetic  25.7 us (5%)
  starting transfers between devices  20.2 us (4%)
  waiting for transfers between devices  7.14 us (2%)
    all_gather x1, blocking collectives, body(): pos_piece = lax.all_gather(marker_pos, 'brick', axis=1, tiled=True)  139 us
    all_gather x1, blocking collectives, body(): force_piece = lax.all_gather(marker_force, 'brick', axis=1, tiled=True)  138 us
    dot_general x8, matrix products, one_block(): jnp.dot(factor, weight_z.astype(jnp.bfloat16), preferred_element_type=jnp...  50 us
    gather x1, local copies, waits for them, and re-layouts, body(): pos = jnp.where(inside, jnp.take(pos_piece, local, axis=1), blank)  31.3 us
    gather x1, local copies, waits for them, and re-layouts, body(): force = jnp.where(inside, jnp.take(force_piece, local, axis=1), blank)  31.2 us
    convert_element_type x8, local copies, waits for them, and re-layouts, one_block(): factor = factor.reshape(3 * cols * rows, block).astype(jnp.bfloat16)  16 us
  transfers between devices with their start and end apart: 6, of which 2 were waited for; matrix products, arithmetic and copies ran while one was open for 0% of the time, Pallas kernels for 0%

commit v1 on v0

--- a/solution.py
+++ b/solution.py
@@ -94,7 +94,15 @@
     blank = jnp.zeros((3, own_slots.shape[0]), jnp.float32)
     start = jnp.int32(0)
     pos_piece = lax.all_gather(marker_pos, "brick", axis=1, tiled=True)
-    force_piece = lax.all_gather(marker_force, "brick", axis=1, tiled=True)
+    ways, here, step = (lax.axis_size("brick"), lax.axis_index("brick"), marker_force.shape[1])
+    line, have = (marker_force, 1)
+    while have < ways:
+        line = jnp.concatenate(
+            [line, lax.ppermute(line, "brick", [(d, (d - have) % ways) for d in range(ways)])],
+            axis=1,
+        )
+        have = 2 * have
+    force_piece = jnp.roll(line, here * step, axis=1)
     length = pos_piece.shape[1]
     inside = ((own_slots >= start) & (own_slots < start + length))[None, :]
     local = jnp.clip(own_slots, 0, length - 1)

time: 470 us -> 354 us (0.75); the launches traced: 469 us -> 348 us
  blocking collectives: 277 us -> 141 us
  local copies, waits for them, and re-layouts: 88.8 us -> 100 us
  matrix products: 50 us -> 57.3 us
    all_gather x1 -> x0, blocking collectives: 138 us -> none  [body(): force_piece = lax.all_gather(marker_force, 'brick', axis=1, tiled=True)]
    dot_general x8, matrix products: 50 us -> 57.3 us  [one_block(): jnp.dot(factor, weight_z.astype(jnp.bfloat16), preferred_element_type=jnp...]
    ppermute x2, waiting for transfers between devices: 7.13 us -> 0.01 us  [extended_2(): lax.ppermute(lax.slice_in_dim(block, 0, width, axis=dim), axis, backward)]
    unnamed x10 -> x43, local copies, waits for them, and re-layouts: 7.83 us -> 14.6 us
  transfers between devices with their start and end apart: 6 -> 8, of which waited for: 2 -> 2; matrix products, arithmetic and copies ran while one was open for 0% -> 12% of each run, Pallas kernels for 0% -> 0%
where the time goes in v1:
time: 354 us; the launch traced here: 348 us
  blocking collectives  141 us (40%)
  local copies, waits for them, and re-layouts  100 us (28%)
  matrix products  57.3 us (16%)
  other arithmetic  27.3 us (8%)
  starting transfers between devices  16.9 us (5%)
  waiting for transfers between devices  4.8 us (1%)
    all_gather x1, blocking collectives, body(): pos_piece = lax.all_gather(marker_pos, 'brick', axis=1, tiled=True)  141 us
    dot_general x8, matrix products, one_block(): jnp.dot(factor, weight_z.astype(jnp.bfloat16), preferred_element_type=jnp...  57.3 us
    gather x1, local copies, waits for them, and re-layouts, body(): pos = jnp.where(inside, jnp.take(pos_piece, local, axis=1), blank)  31.4 us
    gather x1, local copies, waits for them, and re-layouts, body(): force = jnp.where(inside, jnp.take(force_piece, local, axis=1), blank)  31.3 us
    convert_element_type x8, local copies, waits for them, and re-layouts, one_block(): factor = factor.reshape(3 * cols * rows, block).astype(jnp.bfloat16)  15.7 us
    unnamed x43, local copies, waits for them, and re-layouts  14.6 us
    select_n x1, other arithmetic, body(): pos = jnp.where(inside, jnp.take(pos_piece, local, axis=1), blank)  8.05 us
  transfers between devices with their start and end apart: 8, of which 2 were waited for; matrix products, arithmetic and copies ran while one was open for 12% of the time, Pallas kernels for 0%

profile of v1, /device:TPU:19, one launch (start us, length us, event | category | flops | bytes accessed | tf_op | source)
XLA Modules:
  0.0 348.1 jit_solution(3303324852212898019)
XLA Ops:
  0.2 1.5 pad_maximum_fusion.18
  1.7 3.9 %collective-permute-start = (f32[4,1,16,256]{3,2,1,0:T(8,128)}, f32[4,1,16,256]{3,2,1,0:T(8,128)S(1)}, u32[]{:S(2)}, u32[]{:S(2)}) collective-permute-start(f32[4,1,16,256]{3,2,1,0:T(8,128)} %get-tuple-element.221), channel_id=1, source_target_pairs={{0,4},{4,8},{8,12},{12,16},{16,20},{20,24},{24,28},{1,5},{5,9},{9,... | collective-permute-start | bytes 196616 | tf_op jit(solution)/shard_map/ppermute | solution.py:18
  5.6 1.9 collective-permute-start.1
  7.6 1.5 constant_dynamic-update-slice_fusion.5
  9.1 0.8 broadcast_clamp_fusion
  9.9 0.9 and_reduce_fusion
  10.8 2.0 slice_bitcast_fusion.3
  12.8 0.6 copy.21
  13.5 140.8 %all_gather.3 = f32[3,16384]{0,1:T(8,128)} all-gather(f32[3,4096]{0,1:T(8,128)S(1)} %copy.21), channel_id=1, replica_groups=mesh['region'=8,'brick'=4] {'brick'}, dimensions={1}, use_global_device_ids=true | all-gather | bytes 245760 | tf_op jit(solution)/shard_map/all_gather | solution.py:96
  154.3 31.4 %gather_fusion.1 = f32[8192,3]{1,0:T(8,128)} fusion(f32[3,16384]{0,1:T(8,128)} %all_gather.3, s32[8192]{0:T(1024)S(1)} %fusion.44), kind=kCustom, calls=%fused_computation.1.clone | custom fusion | bytes 229376 | tf_op jit(solution)/shard_map/jit(_take)/gather | solution.py:109
  186.0 2.0 collective-permute-start.2
  188.0 3.3 collective-permute-start.3
  191.3 2.7 collective-permute-done.2
  194.0 1.3 select_maximum_fusion
  195.4 1.5 copy-done.2
  196.9 0.9 slice_bitcast_fusion
  198.0 5.1 %copy.24 = f32[3,16384]{0,1:T(8,128)} copy(f32[3,16384]{1,0:T(4,128)S(1)} %constant_dynamic-slice_fusion.2) | data formatting | bytes 393216
  203.1 31.3 %gather_fusion = f32[8192,3]{1,0:T(8,128)} fusion(f32[3,16384]{0,1:T(8,128)} %copy.24, s32[8192]{0:T(1024)S(1)} %copy-done.12), kind=kCustom, calls=%fused_computation.clone | custom fusion | bytes 229376 | tf_op jit(solution)/shard_map/jit(_take)/gather | solution.py:110
  234.4 8.0 %bitcast_select_fusion = (f32[3,8192]{0,1:T(8,128)}, f32[3,8192]{0,1:T(8,128)}) fusion(f32[8192,3]{1,0:T(8,128)} %gather_fusion.1, pred[8192]{0:T(1024)(128)(4,1)S(1)} %compare_and_fusion, pred[8192]{0:T(1024)(128)(4,1)S(1)} %and_reduce_fusion, f32[8192,3]{1,0:T(8,128)} %gather_fusion), kind=kLoop, calls=%fused_computation.47 | loop fusion | flops 98304 | bytes 409600 | tf_op jit(solution)/shard_map/jit(_where)/select_n | solution.py:109
  242.4 2.8 copy.22
  245.3 2.9 copy.23
  248.1 87.1 %while.16 = (s32[]{:T(128)}, f32[960,256]{1,0:T(8,128)}, f32[3,8192]{1,0:T(4,128)S(1)}, f32[3,8192]{1,0:T(4,128)S(1)}, s32[]{:T(128)}, /*index=5*/s32[]{:T(128)}...) while((s32[]{:T(128)}, f32[960,256]{1,0:T(8,128)}, ...), condition=%wide.region_1.3_spmd.clone, body=%wide.region_0.2_spmd.clone.sunk | while | flops 508179072 | bytes 12167789 | solution.py:53
  249.3 0.6 multiply_convert_fusion.2
  249.9 2.0 convert_element_type.63
  251.9 6.9 %convolution_add_fusion.2 = f32[960,256]{1,0:T(8,128)} fusion(bf16[960,1024]{1,0:T(8,128)(2,1)} %convert_element_type.63, f32[960,256]{1,0:T(8,128)} %get-tuple-element.290, f32[1024]{0:T(1024)S(1)} %bitcast.34, f32[256]{0:T(256)S(1)} %convert_add_fusion.8, pred[]{:T(512)S(6)} %compare.36), kind=kOutput, calls=%fused_computation.8.clone.1 | convolution fusion | flops 505905152 | bytes 3937281 | tf_op jit(solution)/shard_map/while/body/eval_jaxpr/dot_general | solution.py:48
  259.9 0.6 multiply_convert_fusion.2
  260.6 2.0 convert_element_type.63
  262.5 7.2 %convolution_add_fusion.2 = f32[960,256]{1,0:T(8,128)} fusion(bf16[960,1024]{1,0:T(8,128)(2,1)} %convert_element_type.63, f32[960,256]{1,0:T(8,128)} %get-tuple-element.290, f32[1024]{0:T(1024)S(1)} %bitcast.34, f32[256]{0:T(256)S(1)} %convert_add_fusion.8, pred[]{:T(512)S(6)} %compare.36), kind=kOutput, calls=%fused_computation.8.clone.1 | convolution fusion | flops 505905152 | bytes 3937281 | tf_op jit(solution)/shard_map/while/body/eval_jaxpr/dot_general | solution.py:48
  270.9 0.6 multiply_convert_fusion.2
  271.5 2.0 convert_element_type.63
  273.4 7.2 %convolution_add_fusion.2 = f32[960,256]{1,0:T(8,128)} fusion(bf16[960,1024]{1,0:T(8,128)(2,1)} %convert_element_type.63, f32[960,256]{1,0:T(8,128)} %get-tuple-element.290, f32[1024]{0:T(1024)S(1)} %bitcast.34, f32[256]{0:T(256)S(1)} %convert_add_fusion.8, pred[]{:T(512)S(6)} %compare.36), kind=kOutput, calls=%fused_computation.8.clone.1 | convolution fusion | flops 505905152 | bytes 3937281 | tf_op jit(solution)/shard_map/while/body/eval_jaxpr/dot_general | solution.py:48
  281.8 0.6 multiply_convert_fusion.2
  282.4 2.0 convert_element_type.63
  284.4 7.2 %convolution_add_fusion.2 = f32[960,256]{1,0:T(8,128)} fusion(bf16[960,1024]{1,0:T(8,128)(2,1)} %convert_element_type.63, f32[960,256]{1,0:T(8,128)} %get-tuple-element.290, f32[1024]{0:T(1024)S(1)} %bitcast.34, f32[256]{0:T(256)S(1)} %convert_add_fusion.8, pred[]{:T(512)S(6)} %compare.36), kind=kOutput, calls=%fused_computation.8.clone.1 | convolution fusion | flops 505905152 | bytes 3937281 | tf_op jit(solution)/shard_map/while/body/eval_jaxpr/dot_general | solution.py:48
  293.3 2.0 convert_element_type.63
  295.3 7.2 %convolution_add_fusion.2 = f32[960,256]{1,0:T(8,128)} fusion(bf16[960,1024]{1,0:T(8,128)(2,1)} %convert_element_type.63, f32[960,256]{1,0:T(8,128)} %get-tuple-element.290, f32[1024]{0:T(1024)S(1)} %bitcast.34, f32[256]{0:T(256)S(1)} %convert_add_fusion.8, pred[]{:T(512)S(6)} %compare.36), kind=kOutput, calls=%fused_computation.8.clone.1 | convolution fusion | flops 505905152 | bytes 3937281 | tf_op jit(solution)/shard_map/while/body/eval_jaxpr/dot_general | solution.py:48
  303.6 0.6 multiply_convert_fusion.2
  304.2 2.0 convert_element_type.63
  306.2 7.2 %convolution_add_fusion.2 = f32[960,256]{1,0:T(8,128)} fusion(bf16[960,1024]{1,0:T(8,128)(2,1)} %convert_element_type.63, f32[960,256]{1,0:T(8,128)} %get-tuple-element.290, f32[1024]{0:T(1024)S(1)} %bitcast.34, f32[256]{0:T(256)S(1)} %convert_add_fusion.8, pred[]{:T(512)S(6)} %compare.36), kind=kOutput, calls=%fused_computation.8.clone.1 | convolution fusion | flops 505905152 | bytes 3937281 | tf_op jit(solution)/shard_map/while/body/eval_jaxpr/dot_general | solution.py:48
  315.2 2.0 convert_element_type.63
  317.1 7.2 %convolution_add_fusion.2 = f32[960,256]{1,0:T(8,128)} fusion(bf16[960,1024]{1,0:T(8,128)(2,1)} %convert_element_type.63, f32[960,256]{1,0:T(8,128)} %get-tuple-element.290, f32[1024]{0:T(1024)S(1)} %bitcast.34, f32[256]{0:T(256)S(1)} %convert_add_fusion.8, pred[]{:T(512)S(6)} %compare.36), kind=kOutput, calls=%fused_computation.8.clone.1 | convolution fusion | flops 505905152 | bytes 3937281 | tf_op jit(solution)/shard_map/while/body/eval_jaxpr/dot_general | solution.py:48
  326.1 2.0 convert_element_type.63
  328.0 7.2 %convolution_add_fusion.2 = f32[960,256]{1,0:T(8,128)} fusion(bf16[960,1024]{1,0:T(8,128)(2,1)} %convert_element_type.63, f32[960,256]{1,0:T(8,128)} %get-tuple-element.290, f32[1024]{0:T(1024)S(1)} %bitcast.34, f32[256]{0:T(256)S(1)} %convert_add_fusion.8, pred[]{:T(512)S(6)} %compare.36), kind=kOutput, calls=%fused_computation.8.clone.1 | convolution fusion | flops 505905152 | bytes 3937281 | tf_op jit(solution)/shard_map/while/body/eval_jaxpr/dot_general | solution.py:48
  335.2 1.4 reshape.182
  336.8 2.2 collective-permute-start.6
  339.5 3.4 collective-permute-start.7
  343.0 2.1 collective-permute-done.7
  345.3 2.8 multiply_add_fusion
  (188 shorter events, 12.0 us)
Async XLA Ops:
  0.0 12.8 %copy-start.20 = (f32[3,4096]{1,0:T(4,128)S(1)}, f32[3,4096]{1,0:T(4,128)}, u32[]{:S(2)}) copy-start(f32[3,4096]{1,0:T(4,128)} %param.15) | copy-start | bytes 147460
  0.0 185.7 %collective-permute-start.4 = (f32[3,4096]{1,0:T(4,128)}, f32[3,4096]{1,0:T(4,128)S(1)}, u32[]{:S(2)}, u32[]{:S(2)}) collective-permute-start(f32[3,4096]{1,0:T(4,128)} %param.16), channel_id=1, source_target_pairs={{0,3},{1,0},{2,1},{3,2},{4,7},{5,4},{6,5},{7,6},{8,11},{9,8},{10,9... | collective-permute-start | bytes 147464 | tf_op jit(solution)/shard_map/ppermute | solution.py:101
  1.7 184.2 %collective-permute-start = (f32[4,1,16,256]{3,2,1,0:T(8,128)}, f32[4,1,16,256]{3,2,1,0:T(8,128)S(1)}, u32[]{:S(2)}, u32[]{:S(2)}) collective-permute-start(f32[4,1,16,256]{3,2,1,0:T(8,128)} %get-tuple-element.221), channel_id=1, source_target_pairs={{0,4},{4,8},{8,12},{12,16},{16,20},{20,24},{24,28},{1,5},{5,9},{9,... | collective-permute-start | bytes 196616 | tf_op jit(solution)/shard_map/ppermute | solution.py:18
  5.6 180.2 %collective-permute-start.1 = (f32[4,1,16,256]{3,2,1,0:T(8,128)}, f32[4,1,16,256]{3,2,1,0:T(8,128)S(1)}, u32[]{:S(2)}, u32[]{:S(2)}) collective-permute-start(f32[4,1,16,256]{3,2,1,0:T(8,128)} %get-tuple-element.222), channel_id=1, source_target_pairs={{4,0},{8,4},{12,8},{16,12},{20,16},{24,20},{28,24},{5,1},{9,5},{13... | collective-permute-start | bytes 196616 | tf_op jit(solution)/shard_map/ppermute | solution.py:21
  9.9 144.4 %copy-start.11 = (s32[8192]{0:T(1024)}, s32[8192]{0:T(1024)S(1)}, u32[]{:S(2)}) copy-start(s32[8192]{0:T(1024)S(1)} %fusion.44) | copy-start | bytes 98308
  13.5 172.3 %copy-start.8 = (f32[3,4096]{1,0:T(4,128)S(1)}, f32[3,4096]{1,0:T(4,128)}, u32[]{:S(2)}) copy-start(f32[3,4096]{1,0:T(4,128)} %param.16) | copy-start | bytes 147460
  13.5 172.4 %copy-start = (f32[3,16,16,256]{3,2,1,0:T(8,128)S(1)}, f32[3,16,16,256]{3,2,1,0:T(8,128)}, u32[]{:S(2)}) copy-start(f32[3,16,16,256]{3,2,1,0:T(8,128)} %param.13) | copy-start | bytes 2359300
  13.5 172.4 %copy-start.4 = (f32[16,16,256]{2,1,0:T(8,128)S(1)}, f32[16,16,256]{2,1,0:T(8,128)}, u32[]{:S(2)}) copy-start(f32[16,16,256]{2,1,0:T(8,128)} %param.14) | copy-start | bytes 786436
  154.3 37.0 %copy-start.19 = (f32[3,32768]{1,0:T(4,128)S(1)}, f32[3,32768]{1,0:T(4,128)}, u32[]{:S(2)}) copy-start(f32[3,32768]{1,0:T(4,128)} %constant_dynamic-update-slice_fusion.5) | copy-start | bytes 1179652
  185.8 12.0 %collective-permute-start.5 = (f32[3,8192]{1,0:T(4,128)S(1)}, f32[3,8192]{1,0:T(4,128)S(1)}, u32[]{:S(2)}, u32[]{:S(2)}) collective-permute-start(f32[3,8192]{1,0:T(4,128)S(1)} %pad_maximum_fusion.12), channel_id=1, source_target_pairs={{0,2},{1,3},{2,0},{3,1},{4,6},{5,7},{6,4},{7,5},{8,10},{9,11},{10,... | collective-permute-start | bytes 294920 | tf_op jit(solution)/shard_map/ppermute | solution.py:101
  186.0 8.0 %collective-permute-start.2 = (f32[4,18,1,256]{3,2,1,0:T(1,128)S(1)}, f32[4,18,1,256]{3,2,1,0:T(1,128)S(1)}, u32[]{:S(2)}, u32[]{:S(2)}) collective-permute-start(f32[4,18,1,256]{3,2,1,0:T(1,128)S(1)} %get-tuple-element.217), channel_id=1, source_target_pairs={{0,1},{1,2},{2,3},{4,5},{5,6},{6,7},{8,9},{9,10},{10,11},{12,13},{... | collective-permute-start | bytes 221192 | tf_op jit(solution)/shard_map/ppermute | solution.py:18
  188.0 6.0 %collective-permute-start.3 = (f32[4,18,1,256]{3,2,1,0:T(1,128)S(1)}, f32[4,18,1,256]{3,2,1,0:T(1,128)S(1)}, u32[]{:S(2)}, u32[]{:S(2)}) collective-permute-start(f32[4,18,1,256]{3,2,1,0:T(1,128)S(1)} %get-tuple-element.218), channel_id=1, source_target_pairs={{1,0},{2,1},{3,2},{5,4},{6,5},{7,6},{9,8},{10,9},{11,10},{13,12},{... | collective-permute-start | bytes 221192 | tf_op jit(solution)/shard_map/ppermute | solution.py:21
  194.0 3.7 %copy-start.13 = (f32[4,18,1,256]{3,2,1,0:T(1,128)}, f32[4,18,1,256]{3,2,1,0:T(1,128)S(1)}, u32[]{:S(2)}) copy-start(f32[4,18,1,256]{3,2,1,0:T(1,128)S(1)} %collective-permute-done.2) | copy-start | bytes 221188
  194.0 3.7 %copy-start.15 = (f32[4,18,1,256]{3,2,1,0:T(1,128)}, f32[4,18,1,256]{3,2,1,0:T(1,128)S(1)}, u32[]{:S(2)}) copy-start(f32[4,18,1,256]{3,2,1,0:T(1,128)S(1)} %collective-permute-done.3) | copy-start | bytes 221188
  195.4 1.5 copy-start.2
  198.0 5.1 %copy-start.12 = (s32[8192]{0:T(1024)S(1)}, s32[8192]{0:T(1024)}, u32[]{:S(2)}) copy-start(s32[8192]{0:T(1024)} %copy-done.11) | copy-start | bytes 98308
  248.1 0.7 copy-start.17
  251.9 7.0 %copy-start.10 = (f32[3,8192]{1,0:T(4,128)S(1)}, f32[3,8192]{1,0:T(4,128)}, u32[]{:S(2)}) copy-start(f32[3,8192]{1,0:T(4,128)} %copy-done.9) | copy-start | bytes 294916 | tf_op jit(solution)/shard_map/while
  251.9 7.0 %copy-start.18 = (f32[3,8192]{1,0:T(4,128)S(1)}, f32[3,8192]{1,0:T(4,128)}, u32[]{:S(2)}) copy-start(f32[3,8192]{1,0:T(4,128)} %copy-done.17) | copy-start | bytes 294916 | tf_op jit(solution)/shard_map/while
  258.8 0.7 copy-start.17
  262.5 7.2 %copy-start.10 = (f32[3,8192]{1,0:T(4,128)S(1)}, f32[3,8192]{1,0:T(4,128)}, u32[]{:S(2)}) copy-start(f32[3,8192]{1,0:T(4,128)} %copy-done.9) | copy-start | bytes 294916 | tf_op jit(solution)/shard_map/while
  262.5 7.2 %copy-start.18 = (f32[3,8192]{1,0:T(4,128)S(1)}, f32[3,8192]{1,0:T(4,128)}, u32[]{:S(2)}) copy-start(f32[3,8192]{1,0:T(4,128)} %copy-done.17) | copy-start | bytes 294916 | tf_op jit(solution)/shard_map/while
  269.7 0.7 copy-start.17
  273.4 7.2 %copy-start.10 = (f32[3,8192]{1,0:T(4,128)S(1)}, f32[3,8192]{1,0:T(4,128)}, u32[]{:S(2)}) copy-start(f32[3,8192]{1,0:T(4,128)} %copy-done.9) | copy-start | bytes 294916 | tf_op jit(solution)/shard_map/while
  273.4 7.2 %copy-start.18 = (f32[3,8192]{1,0:T(4,128)S(1)}, f32[3,8192]{1,0:T(4,128)}, u32[]{:S(2)}) copy-start(f32[3,8192]{1,0:T(4,128)} %copy-done.17) | copy-start | bytes 294916 | tf_op jit(solution)/shard_map/while
  280.6 0.7 copy-start.17
  284.4 7.2 %copy-start.10 = (f32[3,8192]{1,0:T(4,128)S(1)}, f32[3,8192]{1,0:T(4,128)}, u32[]{:S(2)}) copy-start(f32[3,8192]{1,0:T(4,128)} %copy-done.9) | copy-start | bytes 294916 | tf_op jit(solution)/shard_map/while
  284.4 7.2 %copy-start.18 = (f32[3,8192]{1,0:T(4,128)S(1)}, f32[3,8192]{1,0:T(4,128)}, u32[]{:S(2)}) copy-start(f32[3,8192]{1,0:T(4,128)} %copy-done.17) | copy-start | bytes 294916 | tf_op jit(solution)/shard_map/while
  291.6 0.7 copy-start.17
  295.3 7.2 %copy-start.10 = (f32[3,8192]{1,0:T(4,128)S(1)}, f32[3,8192]{1,0:T(4,128)}, u32[]{:S(2)}) copy-start(f32[3,8192]{1,0:T(4,128)} %copy-done.9) | copy-start | bytes 294916 | tf_op jit(solution)/shard_map/while
  295.3 7.2 %copy-start.18 = (f32[3,8192]{1,0:T(4,128)S(1)}, f32[3,8192]{1,0:T(4,128)}, u32[]{:S(2)}) copy-start(f32[3,8192]{1,0:T(4,128)} %copy-done.17) | copy-start | bytes 294916 | tf_op jit(solution)/shard_map/while
  302.5 0.7 copy-start.17
  306.2 7.2 %copy-start.10 = (f32[3,8192]{1,0:T(4,128)S(1)}, f32[3,8192]{1,0:T(4,128)}, u32[]{:S(2)}) copy-start(f32[3,8192]{1,0:T(4,128)} %copy-done.9) | copy-start | bytes 294916 | tf_op jit(solution)/shard_map/while
  306.2 7.2 %copy-start.18 = (f32[3,8192]{1,0:T(4,128)S(1)}, f32[3,8192]{1,0:T(4,128)}, u32[]{:S(2)}) copy-start(f32[3,8192]{1,0:T(4,128)} %copy-done.17) | copy-start | bytes 294916 | tf_op jit(solution)/shard_map/while
  317.1 7.2 %copy-start.10 = (f32[3,8192]{1,0:T(4,128)S(1)}, f32[3,8192]{1,0:T(4,128)}, u32[]{:S(2)}) copy-start(f32[3,8192]{1,0:T(4,128)} %copy-done.9) | copy-start | bytes 294916 | tf_op jit(solution)/shard_map/while
  317.1 7.2 %copy-start.18 = (f32[3,8192]{1,0:T(4,128)S(1)}, f32[3,8192]{1,0:T(4,128)}, u32[]{:S(2)}) copy-start(f32[3,8192]{1,0:T(4,128)} %copy-done.17) | copy-start | bytes 294916 | tf_op jit(solution)/shard_map/while
  324.3 0.7 copy-start.17
  328.0 7.2 %copy-start.10 = (f32[3,8192]{1,0:T(4,128)S(1)}, f32[3,8192]{1,0:T(4,128)}, u32[]{:S(2)}) copy-start(f32[3,8192]{1,0:T(4,128)} %copy-done.9) | copy-start | bytes 294916 | tf_op jit(solution)/shard_map/while
  328.0 7.2 %copy-start.18 = (f32[3,8192]{1,0:T(4,128)S(1)}, f32[3,8192]{1,0:T(4,128)}, u32[]{:S(2)}) copy-start(f32[3,8192]{1,0:T(4,128)} %copy-done.17) | copy-start | bytes 294916 | tf_op jit(solution)/shard_map/while
  335.2 3.7 %copy-start.1 = (f32[18,18,258]{2,1,0:T(8,128)S(1)}, f32[18,18,258]{2,1,0:T(8,128)}, u32[]{:S(2)}) copy-start(f32[18,18,258]{2,1,0:T(8,128)} %slice_bitcast_fusion) | copy-start | bytes 1003108
  336.7 8.5 %copy-start.3 = (f32[4,18,18,258]{3,2,1,0:T(8,128)S(1)}, f32[4,18,18,258]{3,2,1,0:T(8,128)}, u32[]{:S(2)}) copy-start(f32[4,18,18,258]{3,2,1,0:T(8,128)} %copy-done.2) | copy-start | bytes 4012420
  336.7 8.5 %copy-start.5 = (f32[16,16,256]{2,1,0:T(8,128)S(1)}, f32[16,16,256]{2,1,0:T(8,128)}, u32[]{:S(2)}) copy-start(f32[16,16,256]{2,1,0:T(8,128)} %get-tuple-element.223) | copy-start | bytes 786436
  336.7 8.5 %copy-start.6 = (f32[16,16,256]{2,1,0:T(8,128)S(1)}, f32[16,16,256]{2,1,0:T(8,128)}, u32[]{:S(2)}) copy-start(f32[16,16,256]{2,1,0:T(8,128)} %get-tuple-element.224) | copy-start | bytes 786436
  336.7 8.5 %copy-start.7 = (f32[16,16,256]{2,1,0:T(8,128)S(1)}, f32[16,16,256]{2,1,0:T(8,128)}, u32[]{:S(2)}) copy-start(f32[16,16,256]{2,1,0:T(8,128)} %get-tuple-element.225) | copy-start | bytes 786436
  336.7 8.5 %copy-start.14 = (f32[4,18,1,256]{3,2,1,0:T(1,128)S(1)}, f32[4,18,1,256]{3,2,1,0:T(1,128)}, u32[]{:S(2)}) copy-start(f32[4,18,1,256]{3,2,1,0:T(1,128)} %copy-done.13) | copy-start | bytes 221188
  336.7 8.5 %copy-start.16 = (f32[4,18,1,256]{3,2,1,0:T(1,128)S(1)}, f32[4,18,1,256]{3,2,1,0:T(1,128)}, u32[]{:S(2)}) copy-start(f32[4,18,1,256]{3,2,1,0:T(1,128)} %copy-done.15) | copy-start | bytes 221188
  336.8 6.2 %collective-permute-start.6 = (f32[3,16,2,256]{3,2,1,0:T(2,128)S(1)}, f32[3,16,2,256]{3,2,1,0:T(2,128)S(1)}, u32[]{:S(2)}, u32[]{:S(2)}) collective-permute-start(f32[3,16,2,256]{3,2,1,0:T(2,128)S(1)} %get-tuple-element.220), channel_id=1, source_target_pairs={{0,1},{1,2},{2,3},{4,5},{5,6},{6,7},{8,9},{9,10},{10,11},{12,13},{... | collective-permute-start | bytes 294920 | tf_op jit(solution)/shard_map/ppermute | solution.py:10
  339.5 5.6 %collective-permute-start.7 = (f32[3,16,2,256]{3,2,1,0:T(2,128)S(1)}, f32[3,16,2,256]{3,2,1,0:T(2,128)S(1)}, u32[]{:S(2)}, u32[]{:S(2)}) collective-permute-start(f32[3,16,2,256]{3,2,1,0:T(2,128)S(1)} %get-tuple-element.219), channel_id=1, source_target_pairs={{1,0},{2,1},{3,2},{5,4},{6,5},{7,6},{9,8},{10,9},{11,10},{13,12},{... | collective-permute-start | bytes 294920 | tf_op jit(solution)/shard_map/ppermute | solution.py:10
  (9 other events, 5.9 us)
